TPU v7x, 512 devices: a whole 4x4x16 slice. The times are simulated.
512 devices in a mesh: tm: 8 (over x, core), dp: 64 (over z, y).
Axes of the slice: x: 4, y: 4, z: 16, core: 2. Of those that a mesh axis runs over, the one named last changes fastest.
Arguments:
- edge_feat: bfloat16 [8, 8192, 186], P('tm', 'dp'), may hold values from -6 to 6
- endpoint_slots: int32 [8, 2, 8192], P('tm', None, 'dp'), may hold values from 0 to 2047, as said below
- neighbor_slots: int32 [8, 20, 8192], P('tm', None, 'dp'), may hold values from 0 to 2047, as said below
- neighbor_gap: int32 [8, 20, 8192], P('tm', None, 'dp'), may hold values from 0 to 999
- score_grad: float32 [8, 8192], P('tm', 'dp'), may hold values from -1.5 to 1.5
- node_list: int32 [8, 64, 2048], P('tm', 'dp'), may hold values from 0 to 128, as said below
- memory0: float32 [8192, 256], P('dp'), may hold values from -6 to 6
- msg_weight: bfloat16 [186, 256], replicated, may hold values from -0.4375 to 0.4375
- gate_weight: bfloat16 [256, 512], replicated, may hold values from -0.375 to 0.375
- gate_bias: float32 [512], replicated, may hold values from -4 to 4
- omega: float32 [256], replicated, may hold values from 0.001 to 1
- attn_weights: bfloat16 [4, 256, 256], replicated, may hold values from -0.375 to 0.375
- pred_weights: bfloat16 [2, 256, 256], replicated, may hold values from -0.375 to 0.375
- pred_out: float32 [256], replicated, may hold values from -0.375 to 0.375
Outputs:
- scores: float32 [8, 8192], P('tm', 'dp')
- new_memory: float32 [8, 8192, 256], P('tm', 'dp')
- grad_out_proj: float32 [256, 256], replicated
- grad_pred: float32 [2, 256, 256], replicated
Inputs may be any that keep to these rules, and one draw needn't show every extreme that they name: `node_list`: each block of 32 slots (one device's requests to one owner) holds distinct rows first and 128 in the empty slots after them; every block holds at least one row; in each mini-batch some owner's block is full from every device. `endpoint_slots`: every slot points at a non-empty entry of its device's node list. `neighbor_slots`: every slot points at a non-empty entry of its device's node list.
All inputs are finite; a program needn't handle non-finite values.
Results may differ from a plain program's by a relative error of at most 0.017.
Values may be sent and summed in bfloat16 or wider, within the bound.
No kernel may reach another device: no remote copies, remote signals or barrier semaphores. Data moves between devices by JAX's collectives and lax.ppermute only.
A program may use at most 64 MiB of HBM per device.

v0:
```python
import math
import jax
import jax.numpy as jnp
from jax import lax
from jax.sharding import PartitionSpec as P

HEADS = 2


def shifted(value, axis, steps):
    count = lax.axis_size(axis)
    initial, last = (max(0, -steps), min(count, count - steps))
    return lax.ppermute(value, axis, [(source, source + steps) for source in range(initial, last)])


def local_step(
    slot_rows,
    end_slots,
    near_slots,
    near_gaps,
    cot_rows,
    omega,
    attn_weights,
    pred_weights,
    pred_out,
):
    feat_width = slot_rows.shape[1]
    events = end_slots.shape[1]
    near_count = near_slots.shape[0] // 2
    head_dim = feat_width // HEADS
    self_rows = jnp.take(slot_rows, end_slots, axis=0)
    near_rows = jnp.take(slot_rows, near_slots, axis=0).reshape(2, near_count, events, feat_width)
    phases = near_gaps.reshape(2, near_count, events).astype(jnp.float32)[..., None] * omega
    near_feat = (near_rows.astype(jnp.float32) + jnp.cos(phases)).astype(jnp.bfloat16)
    query_proj = jnp.einsum(
        "pea,ab->peb", self_rows, attn_weights[0], preferred_element_type=jnp.float32
    )
    key_proj = jnp.einsum(
        "pkea,ab->pkeb", near_feat, attn_weights[1], preferred_element_type=jnp.float32
    )
    value_proj = jnp.einsum(
        "pkea,ab->pkeb", near_feat, attn_weights[2], preferred_element_type=jnp.float32
    )
    query_heads = query_proj.reshape(2, 1, events, HEADS, head_dim)
    key_heads = key_proj.reshape(2, near_count, events, HEADS, head_dim)
    value_heads = value_proj.reshape(2, near_count, events, HEADS, head_dim)
    att_logits = jnp.sum(query_heads * key_heads, axis=-1) / math.sqrt(head_dim)
    weights_att = jax.nn.softmax(att_logits, axis=1)
    mixed_heads = (
        jnp.sum(weights_att[..., None] * value_heads, axis=1)
        .reshape(2, events, feat_width)
        .astype(jnp.bfloat16)
    )
    state_full = self_rows.astype(jnp.float32) + jnp.einsum(
        "pea,ab->peb", mixed_heads, attn_weights[3], preferred_element_type=jnp.float32
    )
    state_bf = state_full.astype(jnp.bfloat16)
    pre_pred = jnp.dot(state_bf[0], pred_weights[0], preferred_element_type=jnp.float32) + jnp.dot(
        state_bf[1], pred_weights[1], preferred_element_type=jnp.float32
    )
    sigmoid_pre = jax.nn.sigmoid(pre_pred)
    logit_out = jnp.sum(pre_pred * sigmoid_pre * pred_out, axis=-1)
    grad_pre = (
        cot_rows[:, None] * pred_out * (sigmoid_pre * (1.0 + pre_pred * (1.0 - sigmoid_pre)))
    ).astype(jnp.bfloat16)
    grad_first = jnp.einsum("ea,eb->ab", state_bf[0], grad_pre, preferred_element_type=jnp.float32)
    grad_second = jnp.einsum("ea,eb->ab", state_bf[1], grad_pre, preferred_element_type=jnp.float32)
    grad_state = jnp.einsum(
        "eb,pab->pea", grad_pre, pred_weights, preferred_element_type=jnp.float32
    ).astype(jnp.bfloat16)
    grad_out_proj = jnp.einsum(
        "pea,peb->ab", mixed_heads, grad_state, preferred_element_type=jnp.float32
    )
    return (logit_out, grad_out_proj, jnp.stack([grad_first, grad_second]))


def per_device(
    edge_feat,
    endpoint_slots,
    neighbor_slots,
    neighbor_gap,
    score_grad,
    node_list,
    memory0,
    msg_weight,
    gate_weight,
    gate_bias,
    omega,
    attn_weights,
    pred_weights,
    pred_out,
):
    groups = lax.axis_size("dp")
    node_dev, feat_width = memory0.shape
    list_len = node_list.shape[2]
    per_owner = list_len // groups
    requests = node_list[0, 0].reshape(groups, per_owner)
    wanted = lax.all_to_all(requests, "dp", split_axis=0, concat_axis=0, tiled=True)
    message = jnp.dot(edge_feat[0], msg_weight, preferred_element_type=jnp.float32).astype(
        jnp.bfloat16
    )
    message_wide = message.astype(jnp.float32)
    end_slots = endpoint_slots[0]
    flat_ends = end_slots.reshape(-1)
    slot_sums = (
        jnp.zeros((list_len, feat_width), jnp.float32)
        .at[flat_ends]
        .add(jnp.concatenate([message_wide, message_wide]))
    )
    slot_tally = jnp.zeros((list_len,), jnp.float32).at[flat_ends].add(1.0)
    got_sums, got_tally = (
        lax.all_to_all(
            slot_sums.reshape(groups, per_owner, feat_width),
            "dp",
            split_axis=0,
            concat_axis=0,
            tiled=True,
        ),
        lax.all_to_all(
            slot_tally.reshape(groups, per_owner), "dp", split_axis=0, concat_axis=0, tiled=True
        ),
    )
    picker = (wanted.reshape(-1)[:, None] == jnp.arange(node_dev)[None, :]).astype(jnp.bfloat16)
    flat_sums = got_sums.reshape(-1, feat_width)
    sums_high = flat_sums.astype(jnp.bfloat16)
    sums_low = (flat_sums - sums_high.astype(jnp.float32)).astype(jnp.bfloat16)
    totals = jnp.einsum(
        "sn,sd->nd", picker, sums_high, preferred_element_type=jnp.float32
    ) + jnp.einsum("sn,sd->nd", picker, sums_low, preferred_element_type=jnp.float32)
    counts = jnp.dot(
        got_tally.reshape(-1), picker.astype(jnp.float32), precision=lax.Precision.HIGHEST
    )
    touched = (counts > 0.5).astype(jnp.float32)
    mean_msg = (totals / jnp.maximum(counts, 1.0)[:, None]).astype(jnp.bfloat16)
    pre_gate = jnp.dot(mean_msg, gate_weight, preferred_element_type=jnp.float32) + gate_bias
    update = jax.nn.sigmoid(pre_gate[:, :feat_width]) * touched[:, None]
    candidate = jnp.tanh(pre_gate[:, feat_width:])
    decay_rate = 1.0 - update
    inject = update * candidate
    section_index = lax.axis_index("tm")
    before = memory0
    for relay_step in range(lax.axis_size("tm") - 1):
        moved_state = shifted((decay_rate * before + inject).astype(jnp.bfloat16), "tm", 1).astype(
            jnp.float32
        )
        before = jnp.where(section_index == 0, memory0, moved_state)
    new_memory = decay_rate * before + inject
    memory_bf = before.astype(jnp.bfloat16)
    full_table = lax.all_gather(memory_bf, "dp", axis=0, tiled=True)
    owner_of = jnp.arange(list_len, dtype=jnp.int32) // per_owner
    global_row = owner_of * node_dev + jnp.minimum(node_list[0, 0], node_dev - 1)
    slot_rows = jnp.take(full_table, global_row, axis=0)
    logit_out, grad_out, grad_pair = local_step(
        slot_rows,
        end_slots,
        neighbor_slots[0],
        neighbor_gap[0],
        score_grad[0],
        omega,
        attn_weights,
        pred_weights,
        pred_out,
    )
    grad_out, grad_pair = lax.psum((grad_out, grad_pair), ("tm", "dp"))
    return (logit_out[None, :], new_memory[None], grad_out, grad_pair)


def solution(mesh):
    in_specs = (
        P("tm", "dp", None),
        P("tm", None, "dp"),
        P("tm", None, "dp"),
        P("tm", None, "dp"),
        P("tm", "dp"),
        P("tm", "dp", None),
        P("dp", None),
        P(),
        P(),
        P(),
        P(),
        P(),
        P(),
        P(),
    )
    out_specs = (P("tm", "dp"), P("tm", "dp", None), P(), P())
    return jax.shard_map(
        per_device, mesh=mesh, in_specs=in_specs, out_specs=out_specs, check_vma=False
    )
```

profile of v0, /device:TPU:2, one launch (start us, length us, event | category | flops | bytes accessed | tf_op | source)
XLA Modules:
  0.0 856.8 jit_solution(11601709572848172272)
XLA Ops:
  7.7 1.4 broadcast_minimum_fusion
  9.8 18.7 %all-to-all-start = ((s32[64,1,32]{2,1,0:T(1,128)}), s32[64,1,32]{2,1,0:T(1,128)S(1)}, u32[]{:S(2)}, u32[]{:S(2)}) async-start(s32[64,1,32]{2,1,0:T(1,128)} %bitcast.2), calls=%async_computation | async-start | bytes 65536 | tf_op jit(solution)/shard_map/all_to_all | solution.py:98
  29.2 2.0 scatter_custom_fusion.1
  31.8 11.2 %all-to-all-done = s32[64,1,32]{2,1,0:T(1,128)S(1)} async-done(((s32[64,1,32]{2,1,0:T(1,128)}), s32[64,1,32]{2,1,0:T(1,128)S(1)}, u32[]{:S(2)}, u32[]{:S(2)}) %all-to-all-start) | async-done | bytes 8224 | tf_op jit(solution)/shard_map/all_to_all | solution.py:98
  43.0 4.6 all-to-all-start.2
  48.7 3.4 scatter_custom_fusion
  52.1 10.2 %all-to-all-done.2 = f32[64,1,32]{2,1,0:T(1,128)S(1)} async-done(((f32[64,1,32]{2,1,0:T(1,128)}), f32[64,1,32]{2,1,0:T(1,128)S(1)}, u32[]{:S(2)}, u32[]{:S(2)}) %all-to-all-start.2) | async-done | bytes 8224 | tf_op jit(solution)/shard_map/all_to_all | solution.py:119
  62.3 4.9 all-to-all-start.1
  70.0 95.7 %all-to-all-done.1 = f32[64,32,256]{2,1,0:T(8,128)S(1)} async-done(((f32[64,32,256]{2,1,0:T(8,128)}), f32[64,32,256]{2,1,0:T(8,128)S(1)}, u32[]{:S(2)}, u32[]{:S(2)}) %all-to-all-start.1) | async-done | bytes 2097184 | tf_op jit(solution)/shard_map/all_to_all | solution.py:112
  168.0 2.1 collective-permute-start
  170.0 3.6 collective-permute-done
  173.8 1.9 collective-permute-start.1
  175.7 3.7 collective-permute-done.1
  179.5 2.1 collective-permute-start.2
  181.5 3.7 collective-permute-done.2
  185.3 1.9 collective-permute-start.3
  187.2 3.7 collective-permute-done.3
  191.0 1.9 collective-permute-start.4
  192.9 3.7 collective-permute-done.4
  196.7 1.9 collective-permute-start.5
  198.6 3.7 collective-permute-done.5
  202.3 1.9 collective-permute-start.6
  204.3 3.7 collective-permute-done.6
  210.7 136.2 %all-gather.2.cloned.1.call-done = bf16[8192,256]{1,0:T(8,128)(2,1)} async-done(((bf16[128,256]{1,0:T(8,128)(2,1)}), bf16[8192,256]{1,0:T(8,128)(2,1)}) %all-gather.2.cloned.1.call-update) | async-done | bytes 4194320 | tf_op jit(solution)/shard_map/all_gather | solution.py:149
  346.9 9.4 %gather_fusion = bf16[2048,256]{1,0:T(8,128)(2,1)S(1)} fusion(bf16[8192,256]{1,0:T(8,128)(2,1)} %all-gather.2.cloned.1.call-done, s32[2048]{0:T(1024)S(1)} %broadcast_clamp_fusion), kind=kCustom, calls=%fused_computation | custom fusion | bytes 2105344 | tf_op jit(solution)/shard_map/jit(_take)/gather | solution.py:152
  356.7 7.6 gather_fusion.2
  364.3 1.2 gather_fusion.1
  365.8 10.1 %add_convert_fusion = bf16[20,128,256]{2,1,0:T(8,128)(2,1)S(1)} fusion(f32[256]{0:T(256)S(1)} %copy-done.10, f32[20,128]{1,0:T(8,128)S(1)} %bitcast.137, bf16[20,128,256]{2,1,0:T(8,128)(2,1)S(1)} %bitcast.127, pred[20,128]{1,0:T(8,128)(4,1)S(1)} %compare_and_fusion), kind=kLoop, calls=%fused_computation.7 | loop fusion | flops 3276800 | bytes 2635264 | tf_op jit(solution)/shard_map/convert_element_type | solution.py:34
  378.1 1.1 fusion.1
  383.4 463.0 %all-reduce.3.cloned.1.call-done = (f32[256,256]{1,0:T(8,128)}, f32[2,256,256]{2,1,0:T(8,128)}) async-done(((f32[256,256]{1,0:T(8,128)}, f32[2,256,256]{2,1,0:T(8,128)}), (f32[256,256]{1,0:T(8,128)}, f32[2,256,256]{2,1,0:T(8,128)})) %all-reduce.3.cloned.1.call-update) | async-done | bytes 786448 | tf_op jit(solution)/shard_map/psum | solution.py:164
  846.4 1.7 copy.58
  848.1 1.9 copy.59
  (86 shorter events, 18.8 us)
Async XLA Ops:
  7.2 159.7 %copy-start = (bf16[256,512]{1,0:T(8,128)(2,1)S(1)}, bf16[256,512]{1,0:T(8,128)(2,1)}, u32[]{:S(2)}) copy-start(bf16[256,512]{1,0:T(8,128)(2,1)} %param.22) | copy-start | bytes 786436
  9.8 33.3 %all-to-all-start = ((s32[64,1,32]{2,1,0:T(1,128)}), s32[64,1,32]{2,1,0:T(1,128)S(1)}, u32[]{:S(2)}, u32[]{:S(2)}) async-start(s32[64,1,32]{2,1,0:T(1,128)} %bitcast.2), calls=%async_computation | async-start | bytes 65536 | tf_op jit(solution)/shard_map/all_to_all | solution.py:98
  43.0 19.3 %all-to-all-start.2 = ((f32[64,1,32]{2,1,0:T(1,128)}), f32[64,1,32]{2,1,0:T(1,128)S(1)}, u32[]{:S(2)}, u32[]{:S(2)}) async-start(f32[64,1,32]{2,1,0:T(1,128)} %bitcast.8), calls=%async_computation.2 | async-start | bytes 65536 | tf_op jit(solution)/shard_map/all_to_all | solution.py:119
  62.3 103.4 %all-to-all-start.1 = ((f32[64,32,256]{2,1,0:T(8,128)}), f32[64,32,256]{2,1,0:T(8,128)S(1)}, u32[]{:S(2)}, u32[]{:S(2)}) async-start(f32[64,32,256]{2,1,0:T(8,128)} %bitcast.6), calls=%async_computation.1 | async-start | bytes 4194304 | tf_op jit(solution)/shard_map/all_to_all | solution.py:112
  67.2 279.7 %all-gather.2.cloned.1.call-start = ((), (), s32[]{:S(2)}) async-start(), calls=%async_computation.3 | async-start | bytes 4259840 | tf_op jit(solution)/shard_map/all_gather | solution.py:149
  70.0 96.8 %copy-start.11 = (f32[512]{0:T(512)S(1)}, f32[512]{0:T(512)}, u32[]{:S(2)}) copy-start(f32[512]{0:T(512)} %param.23) | copy-start | bytes 6148
  166.0 1.8 copy-start.1
  167.8 41.0 %copy-start.8 = (s32[1,20,128]{2,0,1:T(1,128)S(1)}, s32[1,20,128]{2,0,1:T(1,128)}, u32[]{:S(2)}) copy-start(s32[1,20,128]{2,0,1:T(1,128)} %param.17) | copy-start | bytes 30724
  167.8 41.0 %copy-start.2 = (bf16[4,256,256]{2,1,0:T(8,128)(2,1)S(1)}, bf16[4,256,256]{2,1,0:T(8,128)(2,1)}, u32[]{:S(2)}) copy-start(bf16[4,256,256]{2,1,0:T(8,128)(2,1)} %param.25) | copy-start | bytes 1572868
  168.0 5.7 collective-permute-start
  173.8 5.6 collective-permute-start.1
  179.4 31.1 %copy-start.9 = (s32[1,2,128]{2,1,0:T(2,128)S(1)}, s32[1,2,128]{2,1,0:T(2,128)}, u32[]{:S(2)}) copy-start(s32[1,2,128]{2,1,0:T(2,128)} %param.15) | copy-start | bytes 3076
  179.5 31.1 %copy-start.6 = (s32[1,20,128]{2,0,1:T(1,128)S(1)}, s32[1,20,128]{2,0,1:T(1,128)}, u32[]{:S(2)}) copy-start(s32[1,20,128]{2,0,1:T(1,128)} %param.16) | copy-start | bytes 30724
  179.5 31.2 %copy-start.7 = (s32[1,1,2048]{2,1,0:T(1,128)S(1)}, s32[1,1,2048]{2,1,0:T(1,128)}, u32[]{:S(2)}) copy-start(s32[1,1,2048]{2,1,0:T(1,128)} %param.19) | copy-start | bytes 24580
  179.5 5.7 collective-permute-start.2
  185.3 5.6 collective-permute-start.3
  191.0 5.6 collective-permute-start.4
  196.7 5.6 collective-permute-start.5
  202.3 5.6 collective-permute-start.6
  208.6 637.8 %all-reduce.3.cloned.1.call-start = ((), (), s32[]{:S(2)}) async-start(), calls=%async_computation.4 | async-start | bytes 1572864 | tf_op jit(solution)/shard_map/psum | solution.py:164
  356.7 9.0 %copy-start.10 = (f32[256]{0:T(256)S(1)}, f32[256]{0:T(256)}, u32[]{:S(2)}) copy-start(f32[256]{0:T(256)} %param.24) | copy-start | bytes 3076
  365.5 10.5 %copy-start.4 = (bf16[256,256]{1,0:T(8,128)(2,1)S(1)}, bf16[256,256]{1,0:T(8,128)(2,1)}, u32[]{:S(2)}) copy-start(bf16[256,256]{1,0:T(8,128)(2,1)} %copy.39) | copy-start | bytes 393220
  375.9 0.9 copy-start.3
  376.5 2.7 copy-start.5
  376.8 2.6 copy-start.12
  376.8 3.4 copy-start.13
Sparse Core Ops, SparseCore 0:
  208.7 138.1 all-gather.1
  382.8 463.6 all-reduce.2
where the time goes:
time: 858 us; the launch traced here: 857 us
  waiting for transfers between devices  742 us (86%)
  starting transfers between devices  42.2 us (5%)
  local copies, waits for them, and re-layouts  26.3 us (3%)
  other arithmetic  22.7 us (3%)
  between operations  14.6 us (2%)
  matrix products  9.08 us (1%)
    psum x1, waiting for transfers between devices, per_device(): grad_out, grad_pair = lax.psum((grad_out, grad_pair), ('tm', 'dp'))  463 us
    all_gather x1, waiting for transfers between devices, per_device(): full_table = lax.all_gather(memory_bf, 'dp', axis=0, tiled=True)  136 us
    all_to_all x1, waiting for transfers between devices, per_device(): lax.all_to_all(slot_sums.reshape(groups, per_owner, feat_width), 'dp', sp...  95.7 us
    ppermute x7, waiting for transfers between devices, shifted(): lax.ppermute(value, axis, [(source, source + steps) for source in range(i...  25.6 us
    all_to_all x1, starting transfers between devices, per_device(): lax.all_to_all(requests, 'dp', split_axis=0, concat_axis=0, tiled=True)  18.7 us
  transfers between devices with their start and end apart: 12, of which 12 were waited for; matrix products, arithmetic and copies ran while one was open for 1% of the time, Pallas kernels for 0%

commit v1 on v0

--- a/solution.py
+++ b/solution.py
@@ -161,7 +161,7 @@
         pred_weights,
         pred_out,
     )
-    grad_out, grad_pair = lax.psum((grad_out, grad_pair), ("tm", "dp"))
+    grad_out, grad_pair = lax.psum(lax.psum((grad_out, grad_pair), "dp"), "tm")
     return (logit_out[None, :], new_memory[None], grad_out, grad_pair)
 
 

time: 858 us -> 732 us (0.85)
  the two profiles are of different devices: /device:TPU:2 before, /device:TPU:8 now
where the time goes in v1:
time: 732 us; the launch traced here: 731 us
  waiting for transfers between devices  599 us (82%)
  starting transfers between devices  60 us (8%)
  local copies, waits for them, and re-layouts  26.3 us (4%)
  other arithmetic  22.7 us (3%)
  between operations  14.3 us (2%)
  matrix products  9.07 us (1%)
    psum x2, waiting for transfers between devices, per_device(): grad_out, grad_pair = lax.psum(lax.psum((grad_out, grad_pair), 'dp'), 'tm')  339 us
    all_gather x1, waiting for transfers between devices, per_device(): full_table = lax.all_gather(memory_bf, 'dp', axis=0, tiled=True)  138 us
    all_to_all x1, waiting for transfers between devices, per_device(): lax.all_to_all(slot_sums.reshape(groups, per_owner, feat_width), 'dp', sp...  95.6 us
    ppermute x7, starting transfers between devices, shifted(): lax.ppermute(value, axis, [(source, source + steps) for source in range(i...  29.6 us
    all_to_all x1, starting transfers between devices, per_device(): lax.all_to_all(requests, 'dp', split_axis=0, concat_axis=0, tiled=True)  18.7 us
  transfers between devices with their start and end apart: 13, of which 13 were waited for; matrix products, arithmetic and copies ran while one was open for 2% of the time, Pallas kernels for 0%

profile of v1, /device:TPU:8, one launch (start us, length us, event | category | flops | bytes accessed | tf_op | source)
XLA Modules:
  0.0 731.2 jit_solution(3051501987258591559)
XLA Ops:
  7.7 1.4 broadcast_minimum_fusion
  9.8 18.7 %all-to-all-start = ((s32[64,1,32]{2,1,0:T(1,128)}), s32[64,1,32]{2,1,0:T(1,128)S(1)}, u32[]{:S(2)}, u32[]{:S(2)}) async-start(s32[64,1,32]{2,1,0:T(1,128)} %bitcast.2), calls=%async_computation | async-start | bytes 65536 | tf_op jit(solution)/shard_map/all_to_all | solution.py:98
  29.2 1.9 scatter_custom_fusion.1
  31.8 10.4 %all-to-all-done = s32[64,1,32]{2,1,0:T(1,128)S(1)} async-done(((s32[64,1,32]{2,1,0:T(1,128)}), s32[64,1,32]{2,1,0:T(1,128)S(1)}, u32[]{:S(2)}, u32[]{:S(2)}) %all-to-all-start) | async-done | bytes 8224 | tf_op jit(solution)/shard_map/all_to_all | solution.py:98
  42.2 5.3 all-to-all-start.2
  47.5 1.1 convolution_convert_fusion.1
  48.6 3.4 scatter_custom_fusion
  52.0 9.1 %all-to-all-done.2 = f32[64,1,32]{2,1,0:T(1,128)S(1)} async-done(((f32[64,1,32]{2,1,0:T(1,128)}), f32[64,1,32]{2,1,0:T(1,128)S(1)}, u32[]{:S(2)}, u32[]{:S(2)}) %all-to-all-start.2) | async-done | bytes 8224 | tf_op jit(solution)/shard_map/all_to_all | solution.py:119
  61.1 6.1 all-to-all-start.1
  70.0 95.6 %all-to-all-done.1 = f32[64,32,256]{2,1,0:T(8,128)S(1)} async-done(((f32[64,32,256]{2,1,0:T(8,128)}), f32[64,32,256]{2,1,0:T(8,128)S(1)}, u32[]{:S(2)}, u32[]{:S(2)}) %all-to-all-start.1) | async-done | bytes 2097184 | tf_op jit(solution)/shard_map/all_to_all | solution.py:112
  166.7 1.0 convolution_add_fusion.1
  167.8 1.4 collective-permute-start
  170.2 4.6 collective-permute-start.1
  174.8 0.9 collective-permute-done.1
  175.8 4.8 collective-permute-start.2
  180.7 0.9 collective-permute-done.2
  181.6 4.7 collective-permute-start.3
  187.3 4.7 collective-permute-start.4
  193.0 4.7 collective-permute-start.5
  198.7 4.7 collective-permute-start.6
  207.1 138.5 %all-gather.2.cloned.1.call-done = bf16[8192,256]{1,0:T(8,128)(2,1)} async-done(((bf16[128,256]{1,0:T(8,128)(2,1)}), bf16[8192,256]{1,0:T(8,128)(2,1)}) %all-gather.2.cloned.1.call-update) | async-done | bytes 4194320 | tf_op jit(solution)/shard_map/all_gather | solution.py:149
  345.5 9.4 %gather_fusion = bf16[2048,256]{1,0:T(8,128)(2,1)S(1)} fusion(bf16[8192,256]{1,0:T(8,128)(2,1)} %all-gather.2.cloned.1.call-done, s32[2048]{0:T(1024)S(1)} %broadcast_clamp_fusion), kind=kCustom, calls=%fused_computation | custom fusion | bytes 2105344 | tf_op jit(solution)/shard_map/jit(_take)/gather | solution.py:152
  355.4 7.6 %gather_fusion.2 = bf16[2560,256]{1,0:T(8,128)(2,1)S(1)} fusion(bf16[2048,256]{1,0:T(8,128)(2,1)S(1)} %broadcast_select_fusion, s32[3072]{0:T(1024)S(1)} %pad_clamp_fusion), kind=kCustom, calls=%fused_computation.2 | custom fusion | bytes 2631680 | tf_op jit(solution)/shard_map/jit(_take)/gather | solution.py:32
  362.9 1.2 gather_fusion.1
  364.4 10.1 %add_convert_fusion = bf16[20,128,256]{2,1,0:T(8,128)(2,1)S(1)} fusion(f32[256]{0:T(256)S(1)} %copy-done.10, f32[20,128]{1,0:T(8,128)S(1)} %bitcast.137, bf16[20,128,256]{2,1,0:T(8,128)(2,1)S(1)} %bitcast.127, pred[20,128]{1,0:T(8,128)(4,1)S(1)} %compare_and_fusion), kind=kLoop, calls=%fused_computation.7 | loop fusion | flops 3276800 | bytes 2635264 | tf_op jit(solution)/shard_map/convert_element_type | solution.py:34
  375.4 1.1 multiply_reduce_fusion
  376.7 1.1 fusion.1
  379.3 1.1 convolution_bitcast_fusion.2
  381.3 263.8 %all-reduce.5.cloned.1.call-done = (f32[256,256]{1,0:T(8,128)}, f32[2,256,256]{2,1,0:T(8,128)}) async-done(((f32[256,256]{1,0:T(8,128)}, f32[2,256,256]{2,1,0:T(8,128)}), (f32[256,256]{1,0:T(8,128)}, f32[2,256,256]{2,1,0:T(8,128)})) %all-reduce.5.cloned.1.call-update) | async-done | bytes 786448 | tf_op jit(solution)/shard_map/psum | solution.py:164
  645.9 75.2 %all-reduce.7.cloned.1.call-done = (f32[256,256]{1,0:T(8,128)}, f32[2,256,256]{2,1,0:T(8,128)}) async-done(((f32[256,256]{1,0:T(8,128)}, f32[2,256,256]{2,1,0:T(8,128)}), (f32[256,256]{1,0:T(8,128)}, f32[2,256,256]{2,1,0:T(8,128)})) %all-reduce.7.cloned.1.call-update) | async-done | bytes 786448 | tf_op jit(solution)/shard_map/psum | solution.py:164
  721.1 1.7 copy.60
  722.8 1.9 copy.61
  (89 shorter events, 19.0 us)
Async XLA Ops:
  7.2 159.5 %copy-start = (bf16[256,512]{1,0:T(8,128)(2,1)S(1)}, bf16[256,512]{1,0:T(8,128)(2,1)}, u32[]{:S(2)}) copy-start(bf16[256,512]{1,0:T(8,128)(2,1)} %param.22) | copy-start | bytes 786436
  9.8 32.5 %all-to-all-start = ((s32[64,1,32]{2,1,0:T(1,128)}), s32[64,1,32]{2,1,0:T(1,128)S(1)}, u32[]{:S(2)}, u32[]{:S(2)}) async-start(s32[64,1,32]{2,1,0:T(1,128)} %bitcast.2), calls=%async_computation | async-start | bytes 65536 | tf_op jit(solution)/shard_map/all_to_all | solution.py:98
  42.2 18.9 %all-to-all-start.2 = ((f32[64,1,32]{2,1,0:T(1,128)}), f32[64,1,32]{2,1,0:T(1,128)S(1)}, u32[]{:S(2)}, u32[]{:S(2)}) async-start(f32[64,1,32]{2,1,0:T(1,128)} %bitcast.8), calls=%async_computation.2 | async-start | bytes 65536 | tf_op jit(solution)/shard_map/all_to_all | solution.py:119
  61.1 104.5 %all-to-all-start.1 = ((f32[64,32,256]{2,1,0:T(8,128)}), f32[64,32,256]{2,1,0:T(8,128)S(1)}, u32[]{:S(2)}, u32[]{:S(2)}) async-start(f32[64,32,256]{2,1,0:T(8,128)} %bitcast.6), calls=%async_computation.1 | async-start | bytes 4194304 | tf_op jit(solution)/shard_map/all_to_all | solution.py:112
  67.2 278.3 %all-gather.2.cloned.1.call-start = ((), (), s32[]{:S(2)}) async-start(), calls=%async_computation.3 | async-start | bytes 4259840 | tf_op jit(solution)/shard_map/all_gather | solution.py:149
  70.0 96.7 %copy-start.11 = (f32[512]{0:T(512)S(1)}, f32[512]{0:T(512)}, u32[]{:S(2)}) copy-start(f32[512]{0:T(512)} %param.23) | copy-start | bytes 6148
  165.9 1.8 copy-start.1
  167.7 37.5 %copy-start.8 = (s32[1,20,128]{2,0,1:T(1,128)S(1)}, s32[1,20,128]{2,0,1:T(1,128)}, u32[]{:S(2)}) copy-start(s32[1,20,128]{2,0,1:T(1,128)} %param.17) | copy-start | bytes 30724
  167.7 37.5 %copy-start.2 = (bf16[4,256,256]{2,1,0:T(8,128)(2,1)S(1)}, bf16[4,256,256]{2,1,0:T(8,128)(2,1)}, u32[]{:S(2)}) copy-start(bf16[4,256,256]{2,1,0:T(8,128)(2,1)} %param.25) | copy-start | bytes 1572868
  167.8 2.3 collective-permute-start
  170.2 5.4 collective-permute-start.1
  175.8 31.1 %copy-start.9 = (s32[1,2,128]{2,1,0:T(2,128)S(1)}, s32[1,2,128]{2,1,0:T(2,128)}, u32[]{:S(2)}) copy-start(s32[1,2,128]{2,1,0:T(2,128)} %param.15) | copy-start | bytes 3076
  175.8 31.1 %copy-start.6 = (s32[1,20,128]{2,0,1:T(1,128)S(1)}, s32[1,20,128]{2,0,1:T(1,128)}, u32[]{:S(2)}) copy-start(s32[1,20,128]{2,0,1:T(1,128)} %param.16) | copy-start | bytes 30724
  175.8 31.2 %copy-start.7 = (s32[1,1,2048]{2,1,0:T(1,128)S(1)}, s32[1,1,2048]{2,1,0:T(1,128)}, u32[]{:S(2)}) copy-start(s32[1,1,2048]{2,1,0:T(1,128)} %param.19) | copy-start | bytes 24580
  175.8 5.7 collective-permute-start.2
  181.6 5.6 collective-permute-start.3
  187.3 5.6 collective-permute-start.4
  193.0 5.6 collective-permute-start.5
  198.7 5.6 collective-permute-start.6
  204.9 440.2 %all-reduce.5.cloned.1.call-start = ((), (), s32[]{:S(2)}) async-start(), calls=%async_computation.4 | async-start | bytes 1572864 | tf_op jit(solution)/shard_map/psum | solution.py:164
  355.3 9.0 %copy-start.10 = (f32[256]{0:T(256)S(1)}, f32[256]{0:T(256)}, u32[]{:S(2)}) copy-start(f32[256]{0:T(256)} %param.24) | copy-start | bytes 3076
  364.1 10.5 %copy-start.4 = (bf16[256,256]{1,0:T(8,128)(2,1)S(1)}, bf16[256,256]{1,0:T(8,128)(2,1)}, u32[]{:S(2)}) copy-start(bf16[256,256]{1,0:T(8,128)(2,1)} %copy.39) | copy-start | bytes 393220
  374.5 0.9 copy-start.3
  375.1 2.7 copy-start.5
  375.4 2.5 copy-start.12
  375.4 3.4 copy-start.13
  381.3 339.9 %all-reduce.7.cloned.1.call-start = ((), (), s32[]{:S(2)}) async-start(), calls=%async_computation.5 | async-start | bytes 1572864 | tf_op jit(solution)/shard_map/psum | solution.py:164
Sparse Core Ops, SparseCore 0:
  205.1 140.4 all-gather.1
  381.4 263.6 all-reduce.4
  647.8 73.3 all-reduce.6
